TPU v7x, 512 devices: a whole 4x4x16 slice. The times are simulated.
512 devices in a mesh: row: 64 (over z_hi, x, y), col: 8 (over z_lo, core).
Axes of the slice: x: 4, y: 4, z: 16 (z_hi: 4, z_lo: 4; z = z_hi * 4 + z_lo), core: 2. Of those that a mesh axis runs over, the one named last changes fastest.
Arguments:
- tensor: float32 [8, 8192, 8192], P(None, 'row', 'col'), may hold values from -0.8 to 0.8
- factor_a: float32 [8192, 256], P(('row', 'col')), may hold values from -0.0625 to 0.0625
- factor_bt: float32 [256, 8192], P('row', 'col'), may hold values from -0.0625 to 0.0625
- factor_c: float32 [8, 256], replicated, may hold values from -6 to 6
Outputs:
- grad_a: float32 [8192, 256], P(('row', 'col'))
- grad_bt: float32 [256, 8192], P('row', 'col')
- grad_c: float32 [8, 256], replicated
All inputs are finite; a program needn't handle non-finite values.
Results may differ from a plain program's by a relative error of at most 0.0001.
Values sent between devices are 32-bit elements; how exact they have to be, the bound alone decides.
A program may use at most 64 MiB of HBM per device.

v0:
```python
import jax
import jax.numpy as jnp
from jax import lax
from jax.sharding import PartitionSpec as P


def local(tensor, factor_a, factor_bt, factor_c):
    highest = lax.Precision.HIGHEST
    rank_rows = factor_bt.shape[0]
    block_a = lax.all_gather(factor_a, "col", axis=0, tiled=True)
    gram_c = jnp.dot(factor_c.T, factor_c, precision=highest)
    weighted = block_a[None, :, :] * factor_c[:, None, :]
    block_bt = lax.all_gather(factor_bt, "row", axis=0, tiled=True)
    mttkrp_bt = lax.psum_scatter(
        jnp.einsum("kir,kij->rj", weighted, tensor, precision=highest),
        "row",
        scatter_dimension=0,
        tiled=True,
    )
    contracted = jnp.einsum("kij,rj->kir", tensor, block_bt, precision=highest)
    partial_a = jnp.sum(contracted * factor_c[:, None, :], axis=0)
    partial_c = jnp.sum(contracted * block_a[None, :, :], axis=1)
    mttkrp_a = lax.psum_scatter(partial_a, "col", scatter_dimension=0, tiled=True)
    mttkrp_c = lax.psum(partial_c, ("row", "col"))
    local_gram_a = jnp.dot(factor_a.T, factor_a, precision=highest)
    gram_a = lax.psum(local_gram_a, ("row", "col"))
    gram_b = lax.psum(jnp.dot(block_bt, block_bt.T, precision=highest), "col")
    grad_a = jnp.dot(factor_a, gram_b * gram_c, precision=highest) - mttkrp_a
    h_rows = lax.dynamic_slice_in_dim(
        gram_a * gram_c, lax.axis_index("row") * rank_rows, rank_rows, 0
    )
    grad_bt = jnp.dot(h_rows, block_bt, precision=highest) - mttkrp_bt
    grad_c = jnp.dot(factor_c, gram_a * gram_b, precision=highest) - mttkrp_c
    return (grad_a, grad_bt, grad_c)


def solution(mesh):
    in_specs = (P(None, "row", "col"), P(("row", "col"), None), P("row", "col"), P())
    out_specs = (P(("row", "col"), None), P("row", "col"), P())
    return jax.shard_map(local, mesh=mesh, in_specs=in_specs, out_specs=out_specs, check_vma=False)
```

profile of v0, /device:TPU:2, one launch (start us, length us, event | category | flops | bytes accessed | tf_op | source)
XLA Modules:
  0.0 1439.3 jit_solution(11810171701839936095)
XLA Ops:
  8.0 0.0 all-gather.3.cloned.1.call-start
  8.0 0.7 all-gather.3.cloned.1.call-update
  8.7 0.0 all-reduce.7.cloned.1.call-start
  8.8 1.9 fusion.11
  10.7 0.0 all-reduce.7.cloned.1.call-update
  10.7 0.0 all-reduce.9.cloned.1.call-start
  10.8 15.1 %all_gather.7 = f32[128,256]{1,0:T(8,128)S(1)} all-gather(f32[16,256]{1,0:T(8,128)} %param.5), channel_id=1, replica_groups=mesh['row'=64,'col'=8] {'col'}, dimensions={0}, use_global_device_ids=true | all-gather | bytes 147456 | tf_op jit(solution)/shard_map/all_gather | solution.py:10
  25.9 0.0 copy-start.2
  25.9 6.8 convolution_bitcast_fusion
  32.7 0.0 all-reduce.9.cloned.1.call-update
  32.7 0.0 reduce-scatter.2.cloned.1.call-start
  32.7 89.5 %all-gather.3.cloned.1.call-done = f32[64,4,1024]{2,1,0:T(4,128)} async-done(((f32[1,4,1024]{2,1,0:T(4,128)}), f32[64,4,1024]{2,1,0:T(4,128)}) %all-gather.3.cloned.1.call-update) | async-done | bytes 1048592 | tf_op jit(solution)/shard_map/all_gather | solution.py:13
  122.3 0.0 copy-start
  122.3 1.7 reshape.10
  123.9 0.0 copy-done.2
  124.0 6.3 multiply_reduce_fusion
  130.3 0.0 copy-start.1
  130.3 0.0 reduce-scatter.2.cloned.1.call-update
  130.3 0.0 all-reduce.5.cloned.1.call-start
  130.3 0.0 copy-done
  130.4 0.4 reshape.9
  130.7 1.7 fusion.9
  132.5 0.0 all-reduce.5.cloned.1.call-update
  132.5 0.4 fusion.10
  132.9 1.3 dynamic-slice
  134.9 100.0 %psum.23 = f32[8,256]{1,0:T(8,128)S(1)} all-reduce(f32[8,256]{1,0:T(8,128)S(1)} %get-tuple-element.3), channel_id=1, replica_groups=mesh['row'=64,'col'=8] {'row','col'}, use_global_device_ids=true, to_apply=%region_6.0 | all-reduce | flops 2048 | bytes 16384 | tf_op jit(solution)/shard_map/psum | solution.py:24
  234.8 257.2 %all-reduce.7.cloned.1.call-done = f32[256,256]{1,0:T(8,128)} async-done(((f32[256,256]{1,0:T(8,128)}), f32[256,256]{1,0:T(8,128)}) %all-reduce.7.cloned.1.call-update) | async-done | bytes 262160 | tf_op jit(solution)/shard_map/psum | solution.py:26
  492.0 845.5 %all-reduce.9.cloned.1.call-done = f32[256,1024]{1,0:T(8,128)} async-done(((f32[256,1024]{1,0:T(8,128)}), f32[256,1024]{1,0:T(8,128)}) %all-reduce.9.cloned.1.call-update) | async-done | bytes 1048592
  1337.5 2.0 convolution_subtract_fusion
  1339.5 0.0 reduce-scatter.2.cloned.1.call-done
  1339.5 88.5 %all-reduce.5.cloned.1.call-done = f32[256,256]{1,0:T(8,128)} async-done(((f32[256,256]{1,0:T(8,128)}), f32[256,256]{1,0:T(8,128)}) %all-reduce.5.cloned.1.call-update) | async-done | bytes 262160 | tf_op jit(solution)/shard_map/psum | solution.py:27
  1428.0 0.0 copy-done.1
  1428.0 1.8 fusion
  1429.9 1.9 fusion.1
Async XLA Ops:
  8.0 114.3 %all-gather.3.cloned.1.call-start = ((), (), s32[]{:S(2)}) async-start(), calls=%async_computation.4 | async-start | bytes 1064960 | tf_op jit(solution)/shard_map/all_gather | solution.py:13
  8.7 483.3 %all-reduce.7.cloned.1.call-start = ((), (), s32[]{:S(2)}) async-start(), calls=%async_computation.3 | async-start | bytes 524288 | tf_op jit(solution)/shard_map/psum | solution.py:26
  10.7 1326.8 %all-reduce.9.cloned.1.call-start = ((), (), s32[]{:S(2)}) async-start(), calls=%async_computation.5 | async-start | bytes 2097152
  25.9 98.1 %copy-start.2 = (f32[8,256]{1,0:T(8,128)S(1)}, f32[8,256]{1,0:T(8,128)}, u32[]{:S(2)}) copy-start(f32[8,256]{1,0:T(8,128)} %param.7) | copy-start | bytes 24580
  32.7 1306.8 %reduce-scatter.2.cloned.1.call-start = ((), (), s32[]{:S(2)}) async-start(), calls=%async_computation.2 | async-start | bytes 147456 | tf_op jit(solution)/shard_map/reduce_scatter | solution.py:23
  122.3 8.1 copy-start
  130.3 1297.8 %copy-start.1 = (f32[16,256]{1,0:T(8,128)S(1)}, f32[16,256]{1,0:T(8,128)}, u32[]{:S(2)}) copy-start(f32[16,256]{1,0:T(8,128)} %param.5) | copy-start | bytes 49156
  130.3 1297.7 %all-reduce.5.cloned.1.call-start = ((), (), s32[]{:S(2)}) async-start(), calls=%async_computation.1 | async-start | bytes 524288 | tf_op jit(solution)/shard_map/psum | solution.py:27
Sparse Core Ops, SparseCore 0:
  13.0 109.2 all-gather.2
  130.4 35.3 reduce-scatter.1
Sparse Core Ops, SparseCore 1:
  14.7 477.3 all-reduce.6
  494.8 842.7 all-reduce.8
  1340.3 87.7 all-reduce.4
where the time goes:
time: 1440 us
  waiting for transfers between devices  1280 us (89%)
  blocking collectives  115 us (8%)
  matrix products  22.9 us (2%)
  between operations  16.4 us (1%)
    unnamed x6, waiting for transfers between devices  846 us
    psum x1, waiting for transfers between devices, local(): gram_a = lax.psum(local_gram_a, ('row', 'col'))  257 us
    psum x1, blocking collectives, local(): mttkrp_c = lax.psum(partial_c, ('row', 'col'))  100 us
    all_gather x1, waiting for transfers between devices, local(): block_bt = lax.all_gather(factor_bt, 'row', axis=0, tiled=True)  89.5 us
    psum x1, waiting for transfers between devices, local(): gram_b = lax.psum(jnp.dot(block_bt, block_bt.T, precision=highest), 'col')  88.5 us
  transfers between devices with their start and end apart: 5, of which 4 were waited for; matrix products, arithmetic and copies ran while one was open for 2% of the time, Pallas kernels for 0%

commit v1 on v0

--- a/solution.py
+++ b/solution.py
@@ -23,7 +23,7 @@
     mttkrp_a = lax.psum_scatter(partial_a, "col", scatter_dimension=0, tiled=True)
     mttkrp_c = lax.psum(partial_c, ("row", "col"))
     local_gram_a = jnp.dot(factor_a.T, factor_a, precision=highest)
-    gram_a = lax.psum(local_gram_a, ("row", "col"))
+    gram_a = lax.psum(lax.psum(local_gram_a, "col"), "row")
     gram_b = lax.psum(jnp.dot(block_bt, block_bt.T, precision=highest), "col")
     grad_a = jnp.dot(factor_a, gram_b * gram_c, precision=highest) - mttkrp_a
     h_rows = lax.dynamic_slice_in_dim(

time: 1440 us -> 1100 us (0.76)
  the two profiles are of different devices: /device:TPU:2 before, /device:TPU:16 now
where the time goes in v1:
time: 1100 us
  waiting for transfers between devices  938 us (85%)
  blocking collectives  118 us (11%)
  matrix products  22.8 us (2%)
  between operations  14.5 us (1%)
    unnamed x5, waiting for transfers between devices  778 us
    all_gather x1, waiting for transfers between devices, local(): block_bt = lax.all_gather(factor_bt, 'row', axis=0, tiled=True)  111 us
    psum x1, blocking collectives, local(): mttkrp_c = lax.psum(partial_c, ('row', 'col'))  104 us
    psum x1, waiting for transfers between devices, local(): gram_b = lax.psum(jnp.dot(block_bt, block_bt.T, precision=highest), 'col')  49.4 us
  transfers between devices with their start and end apart: 4, of which 3 were waited for; matrix products, arithmetic and copies ran while one was open for 2% of the time, Pallas kernels for 0%

profile of v1, /device:TPU:16, one launch (start us, length us, event | category | flops | bytes accessed | tf_op | source)
XLA Modules:
  0.0 1097.1 jit_solution(5120578974710595323)
XLA Ops:
  7.2 0.0 copy-start.1
  7.2 0.0 copy-start.2
  7.2 0.0 all-gather.3.cloned.1.call-start
  7.2 0.7 all-gather.3.cloned.1.call-update
  7.9 0.0 all-reduce.8.cloned.1.call-start
  8.0 1.9 fusion.11
  9.9 111.2 %all-gather.3.cloned.1.call-done = f32[64,4,1024]{2,1,0:T(4,128)} async-done(((f32[1,4,1024]{2,1,0:T(4,128)}), f32[64,4,1024]{2,1,0:T(4,128)}) %all-gather.3.cloned.1.call-update) | async-done | bytes 1048592 | tf_op jit(solution)/shard_map/all_gather | solution.py:13
  121.1 0.0 copy-start
  121.1 1.7 reshape.9
  122.8 1.7 fusion.9
  124.5 0.0 all-reduce.8.cloned.1.call-update
  124.5 0.0 reduce-scatter.2.cloned.1.call-start
  124.6 0.0 copy-done.1
  124.6 14.0 %all_gather.7 = f32[128,256]{1,0:T(8,128)S(1)} all-gather(f32[16,256]{1,0:T(8,128)S(1)} %copy-done.1), channel_id=1, replica_groups=mesh['row'=64,'col'=8] {'col'}, dimensions={0}, use_global_device_ids=true | all-gather | bytes 147456 | tf_op jit(solution)/shard_map/all_gather | solution.py:10
  138.6 0.0 copy-done
  138.6 0.4 reshape.10
  138.9 0.0 copy-done.2
  138.9 6.3 multiply_reduce_fusion
  145.3 0.0 reduce-scatter.2.cloned.1.call-update
  145.3 0.0 all-reduce.6.cloned.1.call-start
  145.3 6.7 convolution_bitcast_fusion
  152.0 49.4 %all-reduce.8.cloned.1.call-done = (f32[256,256]{1,0:T(8,128)}, f32[256,256]{1,0:T(8,128)}) async-done(((f32[256,256]{1,0:T(8,128)}, f32[256,256]{1,0:T(8,128)}), (f32[256,256]{1,0:T(8,128)}, f32[256,256]{1,0:T(8,128)})) %all-reduce.8.cloned.1.call-update) | async-done | bytes 524304 | tf_op jit(solution)/shard_map/psum | solution.py:27
  201.4 0.0 all-reduce.6.cloned.1.call-update
  201.5 1.3 dynamic-slice
  203.4 0.4 fusion.10
  203.8 104.3 %psum.31 = f32[8,256]{1,0:T(8,128)S(1)} all-reduce(f32[8,256]{1,0:T(8,128)S(1)} %get-tuple-element.3), channel_id=1, replica_groups=mesh['row'=64,'col'=8] {'row','col'}, use_global_device_ids=true, to_apply=%region_7.0 | all-reduce | flops 2048 | bytes 16384 | tf_op jit(solution)/shard_map/psum | solution.py:24
  308.1 0.0 reduce-scatter.2.cloned.1.call-done
  308.1 1.8 fusion
  309.9 776.8 %all-reduce.6.cloned.1.call-done = (f32[256,1024]{1,0:T(8,128)}, f32[256,256]{1,0:T(8,128)}) async-done(((f32[256,1024]{1,0:T(8,128)}, f32[256,256]{1,0:T(8,128)}), (f32[256,1024]{1,0:T(8,128)}, f32[256,256]{1,0:T(8,128)})) %all-reduce.6.cloned.1.call-update) | async-done | bytes 1310736
  1086.7 1.9 fusion.1
  1088.6 2.0 convolution_subtract_fusion
Async XLA Ops:
  7.2 117.4 %copy-start.1 = (f32[16,256]{1,0:T(8,128)S(1)}, f32[16,256]{1,0:T(8,128)}, u32[]{:S(2)}) copy-start(f32[16,256]{1,0:T(8,128)} %param.5) | copy-start | bytes 49156
  7.2 131.7 %copy-start.2 = (f32[8,256]{1,0:T(8,128)S(1)}, f32[8,256]{1,0:T(8,128)}, u32[]{:S(2)}) copy-start(f32[8,256]{1,0:T(8,128)} %param.7) | copy-start | bytes 24580
  7.2 113.9 %all-gather.3.cloned.1.call-start = ((), (), s32[]{:S(2)}) async-start(), calls=%async_computation.2 | async-start | bytes 1064960 | tf_op jit(solution)/shard_map/all_gather | solution.py:13
  7.9 193.5 %all-reduce.8.cloned.1.call-start = ((), (), s32[]{:S(2)}) async-start(), calls=%async_computation.4 | async-start | bytes 1048576 | tf_op jit(solution)/shard_map/psum | solution.py:27
  121.1 17.5 %copy-start = (f32[64,4,1024]{2,1,0:T(4,128)S(1)}, f32[64,4,1024]{2,1,0:T(4,128)}, u32[]{:S(2)}) copy-start(f32[64,4,1024]{2,1,0:T(4,128)} %all-gather.3.cloned.1.call-done) | copy-start | bytes 3145732
  124.5 183.6 %reduce-scatter.2.cloned.1.call-start = ((), (), s32[]{:S(2)}) async-start(), calls=%async_computation.1 | async-start | bytes 147456 | tf_op jit(solution)/shard_map/reduce_scatter | solution.py:23
  145.3 941.4 %all-reduce.6.cloned.1.call-start = ((), (), s32[]{:S(2)}) async-start(), calls=%async_computation.3 | async-start | bytes 2621440
Sparse Core Ops, SparseCore 0:
  12.2 108.8 all-gather.2
  124.7 76.7 all-reduce.7
  204.2 40.2 reduce-scatter.1
  247.3 839.3 all-reduce.5

commit v2 on v0

--- a/solution.py
+++ b/solution.py
@@ -10,7 +10,9 @@
     block_a = lax.all_gather(factor_a, "col", axis=0, tiled=True)
     gram_c = jnp.dot(factor_c.T, factor_c, precision=highest)
     weighted = block_a[None, :, :] * factor_c[:, None, :]
-    block_bt = lax.all_gather(factor_bt, "row", axis=0, tiled=True)
+    block_bt = jnp.concatenate(
+        lax.all_to_all(jnp.stack([factor_bt] * lax.axis_size("row")), "row", 0, 0), axis=0
+    )
     mttkrp_bt = lax.psum_scatter(
         jnp.einsum("kir,kij->rj", weighted, tensor, precision=highest),
         "row",

time: 1440 us -> 1460 us (1.014)
  blocking collectives: 115 us -> 158 us
  waiting for transfers between devices: 1280 us -> 1240 us
  starting transfers between devices: 0.21 us -> 21.4 us
    all_gather x1 -> x0, waiting for transfers between devices: 89.5 us -> none  [local(): block_bt = lax.all_gather(factor_bt, 'row', axis=0, tiled=True)]
    psum x1, waiting for transfers between devices: 257 us -> 302 us  [local(): gram_a = lax.psum(local_gram_a, ('row', 'col'))]
    all_gather x1, blocking collectives: 15.1 us -> 51.7 us  [local(): block_a = lax.all_gather(factor_a, 'col', axis=0, tiled=True)]
    all_to_all x0 -> x1, starting transfers between devices: none -> 21.3 us  [local(): lax.all_to_all(jnp.stack([factor_bt] * lax.axis_size('row')), 'row', 0, 0)]
    unnamed x6 -> x5, waiting for transfers between devices: 846 us -> 846 us
  transfers between devices with their start and end apart: 5 -> 5, of which waited for: 4 -> 3; matrix products, arithmetic and copies ran while one was open for 2% -> 1% of each run, Pallas kernels for 0% -> 0%
where the time goes in v2:
time: 1460 us
  waiting for transfers between devices  1240 us (85%)
  blocking collectives  158 us (11%)
  matrix products  22.9 us (2%)
  starting transfers between devices  21.4 us (1%)
  between operations  15.9 us (1%)
    unnamed x5, waiting for transfers between devices  846 us
    psum x1, waiting for transfers between devices, local(): gram_a = lax.psum(local_gram_a, ('row', 'col'))  302 us
    psum x1, blocking collectives, local(): mttkrp_c = lax.psum(partial_c, ('row', 'col'))  106 us
    psum x1, waiting for transfers between devices, local(): gram_b = lax.psum(jnp.dot(block_bt, block_bt.T, precision=highest), 'col')  88.9 us
    all_gather x1, blocking collectives, local(): block_a = lax.all_gather(factor_a, 'col', axis=0, tiled=True)  51.7 us
  transfers between devices with their start and end apart: 5, of which 3 were waited for; matrix products, arithmetic and copies ran while one was open for 1% of the time, Pallas kernels for 0%

profile of v2, /device:TPU:2, one launch (start us, length us, event | category | flops | bytes accessed | tf_op | source)
XLA Modules:
  0.0 1459.2 jit_solution(17608364075125364624)
XLA Ops:
  8.0 2.0 stack.2
  10.0 21.3 %all-to-all-start = ((f32[64,4,1024]{2,1,0:T(4,128)}), f32[64,4,1024]{2,1,0:T(4,128)S(1)}, u32[]{:S(2)}, u32[]{:S(2)}) async-start(f32[64,4,1024]{2,1,0:T(4,128)} %stack.2), calls=%async_computation | async-start | bytes 2097152 | tf_op jit(solution)/shard_map/all_to_all | solution.py:14
  31.2 0.0 all-reduce.7.cloned.1.call-start
  31.3 1.9 fusion.11
  33.2 0.0 all-reduce.7.cloned.1.call-update
  33.2 0.0 all-reduce.9.cloned.1.call-start
  33.3 51.7 %all_gather.3 = f32[128,256]{1,0:T(8,128)S(1)} all-gather(f32[16,256]{1,0:T(8,128)} %param.5), channel_id=1, replica_groups=mesh['row'=64,'col'=8] {'col'}, dimensions={0}, use_global_device_ids=true | all-gather | bytes 147456 | tf_op jit(solution)/shard_map/all_gather | solution.py:10
  84.9 0.0 copy-start.1
  84.9 6.8 convolution_bitcast_fusion
  91.7 0.0 all-reduce.9.cloned.1.call-update
  91.8 0.0 reduce-scatter.2.cloned.1.call-start
  91.8 0.0 all-to-all-done
  91.8 0.4 reshape.14
  92.2 0.0 copy-done.1
  92.2 6.3 multiply_reduce_fusion
  98.5 0.0 copy-start
  98.5 0.0 reduce-scatter.2.cloned.1.call-update
  98.6 0.0 all-reduce.5.cloned.1.call-start
  98.6 0.4 reshape.13
  99.0 1.7 fusion.9
  100.7 0.0 all-reduce.5.cloned.1.call-update
  100.7 0.4 fusion.10
  101.2 1.3 dynamic-slice
  103.1 106.0 %psum.23 = f32[8,256]{1,0:T(8,128)S(1)} all-reduce(f32[8,256]{1,0:T(8,128)S(1)} %get-tuple-element.3), channel_id=1, replica_groups=mesh['row'=64,'col'=8] {'row','col'}, use_global_device_ids=true, to_apply=%region_6.0 | all-reduce | flops 2048 | bytes 16384 | tf_op jit(solution)/shard_map/psum | solution.py:26
  209.1 302.3 %all-reduce.7.cloned.1.call-done = f32[256,256]{1,0:T(8,128)} async-done(((f32[256,256]{1,0:T(8,128)}), f32[256,256]{1,0:T(8,128)}) %all-reduce.7.cloned.1.call-update) | async-done | bytes 262160 | tf_op jit(solution)/shard_map/psum | solution.py:28
  511.4 846.1 %all-reduce.9.cloned.1.call-done = f32[256,1024]{1,0:T(8,128)} async-done(((f32[256,1024]{1,0:T(8,128)}), f32[256,1024]{1,0:T(8,128)}) %all-reduce.9.cloned.1.call-update) | async-done | bytes 1048592
  1357.5 2.0 convolution_subtract_fusion
  1359.5 0.0 reduce-scatter.2.cloned.1.call-done
  1359.5 88.9 %all-reduce.5.cloned.1.call-done = f32[256,256]{1,0:T(8,128)} async-done(((f32[256,256]{1,0:T(8,128)}), f32[256,256]{1,0:T(8,128)}) %all-reduce.5.cloned.1.call-update) | async-done | bytes 262160 | tf_op jit(solution)/shard_map/psum | solution.py:29
  1448.4 0.0 copy-done
  1448.4 1.8 fusion
  1450.2 1.9 fusion.1
Async XLA Ops:
  10.0 81.9 %all-to-all-start = ((f32[64,4,1024]{2,1,0:T(4,128)}), f32[64,4,1024]{2,1,0:T(4,128)S(1)}, u32[]{:S(2)}, u32[]{:S(2)}) async-start(f32[64,4,1024]{2,1,0:T(4,128)} %stack.2), calls=%async_computation | async-start | bytes 2097152 | tf_op jit(solution)/shard_map/all_to_all | solution.py:14
  31.2 480.2 %all-reduce.7.cloned.1.call-start = ((), (), s32[]{:S(2)}) async-start(), calls=%async_computation.4 | async-start | bytes 524288 | tf_op jit(solution)/shard_map/psum | solution.py:28
  33.2 1324.3 %all-reduce.9.cloned.1.call-start = ((), (), s32[]{:S(2)}) async-start(), calls=%async_computation.5 | async-start | bytes 2097152
  84.9 7.3 copy-start.1
  91.8 1267.7 %reduce-scatter.2.cloned.1.call-start = ((), (), s32[]{:S(2)}) async-start(), calls=%async_computation.3 | async-start | bytes 147456 | tf_op jit(solution)/shard_map/reduce_scatter | solution.py:25
  98.5 1349.9 %copy-start = (f32[16,256]{1,0:T(8,128)S(1)}, f32[16,256]{1,0:T(8,128)}, u32[]{:S(2)}) copy-start(f32[16,256]{1,0:T(8,128)} %param.5) | copy-start | bytes 49156
  98.6 1349.8 %all-reduce.5.cloned.1.call-start = ((), (), s32[]{:S(2)}) async-start(), calls=%async_computation.2 | async-start | bytes 524288 | tf_op jit(solution)/shard_map/psum | solution.py:29
Sparse Core Ops, SparseCore 0:
  37.5 473.8 all-reduce.6
  514.3 843.1 all-reduce.8
  1360.4 87.9 all-reduce.4
Sparse Core Ops, SparseCore 1:
  98.7 42.0 reduce-scatter.1

commit v3 on v0

--- a/solution.py
+++ b/solution.py
@@ -24,7 +24,9 @@
     mttkrp_c = lax.psum(partial_c, ("row", "col"))
     local_gram_a = jnp.dot(factor_a.T, factor_a, precision=highest)
     gram_a = lax.psum(local_gram_a, ("row", "col"))
-    gram_b = lax.psum(jnp.dot(block_bt, block_bt.T, precision=highest), "col")
+    gram_b = jnp.sum(
+        lax.all_gather(jnp.dot(block_bt, block_bt.T, precision=highest), "col"), axis=0
+    )
     grad_a = jnp.dot(factor_a, gram_b * gram_c, precision=highest) - mttkrp_a
     h_rows = lax.dynamic_slice_in_dim(
         gram_a * gram_c, lax.axis_index("row") * rank_rows, rank_rows, 0

time: 1440 us -> 1360 us (0.944)
  the two profiles are of different devices: /device:TPU:2 before, /device:TPU:8 now
where the time goes in v3:
time: 1360 us
  waiting for transfers between devices  1200 us (88%)
  blocking collectives  116 us (9%)
  matrix products  21.6 us (2%)
  between operations  15.9 us (1%)
    unnamed x6, waiting for transfers between devices  852 us
    psum x1, waiting for transfers between devices, local(): gram_a = lax.psum(local_gram_a, ('row', 'col'))  257 us
    psum x1, blocking collectives, local(): mttkrp_c = lax.psum(partial_c, ('row', 'col'))  101 us
    all_gather x1, waiting for transfers between devices, local(): block_bt = lax.all_gather(factor_bt, 'row', axis=0, tiled=True)  89.4 us
  transfers between devices with their start and end apart: 5, of which 3 were waited for; matrix products, arithmetic and copies ran while one was open for 2% of the time, Pallas kernels for 0%

profile of v3, /device:TPU:8, one launch (start us, length us, event | category | flops | bytes accessed | tf_op | source)
XLA Modules:
  0.0 1357.0 jit_solution(2287250758616800934)
XLA Ops:
  8.0 0.0 all-gather.7.cloned.1.call-start
  8.0 0.7 all-gather.7.cloned.1.call-update
  8.7 0.0 all-reduce.4.cloned.1.call-start
  8.8 1.9 fusion.11
  10.7 0.0 all-reduce.4.cloned.1.call-update
  10.7 0.0 all-reduce.6.cloned.1.call-start
  10.8 15.1 %all_gather.15 = f32[128,256]{1,0:T(8,128)S(1)} all-gather(f32[16,256]{1,0:T(8,128)} %param.5), channel_id=1, replica_groups=mesh['row'=64,'col'=8] {'col'}, dimensions={0}, use_global_device_ids=true | all-gather | bytes 147456 | tf_op jit(solution)/shard_map/all_gather | solution.py:10
  25.9 6.7 convolution_bitcast_fusion
  32.6 0.0 copy-start.3
  32.6 0.0 all-reduce.6.cloned.1.call-update
  32.6 0.0 all-gather.5.cloned.1.call-start
  32.7 89.4 %all-gather.7.cloned.1.call-done = f32[64,4,1024]{2,1,0:T(4,128)} async-done(((f32[1,4,1024]{2,1,0:T(4,128)}), f32[64,4,1024]{2,1,0:T(4,128)}) %all-gather.7.cloned.1.call-update) | async-done | bytes 1048592 | tf_op jit(solution)/shard_map/all_gather | solution.py:13
  122.1 0.0 copy-start
  122.1 1.7 reshape.10
  123.8 1.7 fusion.9
  125.5 0.0 all-gather.5.cloned.1.call-update
  125.6 0.0 reduce-scatter.2.cloned.1.call-start
  125.6 0.0 copy-done
  125.6 0.4 reshape.11
  126.0 0.0 copy-done.3
  126.0 0.0 copy-start.2
  126.0 6.3 multiply_reduce_fusion
  132.4 0.0 reduce-scatter.2.cloned.1.call-update
  132.4 0.4 fusion.10
  132.8 1.3 dynamic-slice
  134.8 100.7 %psum.15 = f32[8,256]{1,0:T(8,128)S(1)} all-reduce(f32[8,256]{1,0:T(8,128)S(1)} %get-tuple-element.3), channel_id=1, replica_groups=mesh['row'=64,'col'=8] {'row','col'}, use_global_device_ids=true, to_apply=%region_6.0 | all-reduce | flops 2048 | bytes 16384 | tf_op jit(solution)/shard_map/psum | solution.py:24
  235.4 256.6 %all-reduce.4.cloned.1.call-done = f32[256,256]{1,0:T(8,128)} async-done(((f32[256,256]{1,0:T(8,128)}), f32[256,256]{1,0:T(8,128)}) %all-reduce.4.cloned.1.call-update) | async-done | bytes 262160 | tf_op jit(solution)/shard_map/psum | solution.py:26
  492.0 0.0 copy-start.1
  492.0 851.6 %all-reduce.6.cloned.1.call-done = f32[256,1024]{1,0:T(8,128)} async-done(((f32[256,1024]{1,0:T(8,128)}), f32[256,1024]{1,0:T(8,128)}) %all-reduce.6.cloned.1.call-update) | async-done | bytes 1048592
  1343.6 2.0 convolution_subtract_fusion
  1345.6 0.0 all-gather.5.cloned.1.call-done
  1345.6 1.8 reduce_sum.27
  1347.4 0.0 reduce-scatter.2.cloned.1.call-done
  1347.4 0.0 copy-done.2
  1347.4 1.6 fusion
  1349.0 0.0 copy-done.1
  1349.0 0.9 fusion.1
Async XLA Ops:
  8.0 114.1 %all-gather.7.cloned.1.call-start = ((), (), s32[]{:S(2)}) async-start(), calls=%async_computation.4 | async-start | bytes 1064960 | tf_op jit(solution)/shard_map/all_gather | solution.py:13
  8.7 483.3 %all-reduce.4.cloned.1.call-start = ((), (), s32[]{:S(2)}) async-start(), calls=%async_computation.2 | async-start | bytes 524288 | tf_op jit(solution)/shard_map/psum | solution.py:26
  10.7 1332.9 %all-reduce.6.cloned.1.call-start = ((), (), s32[]{:S(2)}) async-start(), calls=%async_computation.5 | async-start | bytes 2097152
  32.6 93.4 %copy-start.3 = (f32[8,256]{1,0:T(8,128)S(1)}, f32[8,256]{1,0:T(8,128)}, u32[]{:S(2)}) copy-start(f32[8,256]{1,0:T(8,128)} %param.7) | copy-start | bytes 24580
  32.6 1313.0 %all-gather.5.cloned.1.call-start = ((), (), s32[]{:S(2)}) async-start(), calls=%async_computation.3 | async-start | bytes 2359296 | tf_op jit(solution)/shard_map/all_gather | solution.py:28
  122.1 3.5 copy-start
  125.6 1221.8 %reduce-scatter.2.cloned.1.call-start = ((), (), s32[]{:S(2)}) async-start(), calls=%async_computation.1 | async-start | bytes 147456 | tf_op jit(solution)/shard_map/reduce_scatter | solution.py:23
  126.0 1221.4 %copy-start.2 = (f32[16,256]{1,0:T(8,128)S(1)}, f32[16,256]{1,0:T(8,128)}, u32[]{:S(2)}) copy-start(f32[16,256]{1,0:T(8,128)} %param.5) | copy-start | bytes 49156
  492.0 857.0 %copy-start.1 = (f32[256,256]{1,0:T(8,128)S(1)}, f32[256,256]{1,0:T(8,128)}, u32[]{:S(2)}) copy-start(f32[256,256]{1,0:T(8,128)} %all-reduce.4.cloned.1.call-done) | copy-start | bytes 786436
Sparse Core Ops, SparseCore 0:
  13.0 109.0 all-gather.6
  125.7 38.3 all-gather.4
  166.8 40.8 reduce-scatter.1
Sparse Core Ops, SparseCore 1:
  14.7 477.3 all-reduce.3
  494.8 848.8 all-reduce.5
